TPU v7x, 32 devices: a whole 2x2x4 slice. The times are simulated.
32 devices in a mesh: dp: 16 (over z, y, core), grp: 2 (over x).
Axes of the slice: x: 2, y: 2, z: 4, core: 2. Of those that a mesh axis runs over, the one named last changes fastest.
Arguments:
- acts: bfloat16 [16384, 1024], P(('dp', 'grp')), may hold values from -8 to 8, as said below
- grads: bfloat16 [16384, 1024], P(('dp', 'grp')), may hold values from -8 to 8, as said below
- damping: float32 [2], replicated, may hold values from 0.02 to 0.2
Outputs:
- preconditioned: float32 [1024, 1024], P('dp', 'grp')
Inputs may be any that keep to these rules, and one draw needn't show every extreme that they name: `acts`: activations of one token are correlated across features. `grads`: output gradients are correlated with the activations.
All inputs are finite; a program needn't handle non-finite values. Where the computation divides by a largest or mean magnitude, that divisor is 1e-20 or more.
Results may differ from a plain program's by a relative error of at most 0.0003.
Values sent between devices are 32-bit elements; how exact they have to be, the bound alone decides.
A program may use at most 64 MiB of HBM per device.

v0:
```python
import functools

import jax
import jax.numpy as jnp
from jax import lax
from jax.experimental import pallas as pl
from jax.experimental.pallas import tpu as pltpu
from jax.sharding import PartitionSpec as P

LANES = 128
PANEL = 256
MESH = pl.DeviceIdType.MESH


def kernel(
    nz, nx, scale, damping, acts, grads, out,
    mat, cross, stack, flipped, outgoing, incoming, own,
    sum_e, sum_o, got_e1, got_e2, got_o1, got_o2, pair, got_z, mine,
    full, high, low, block, wide, turned, landed, parted,
    send_sem, recv_sem, turn_send, turn_recv, part_send, part_recv,
):
    dp = lax.axis_index("dp")
    x = lax.axis_index("grp")
    core = lax.rem(dp, 2)
    y = lax.rem(dp // 2, 2)
    z = dp // 4
    other = 1 - core
    width = acts.shape[1]
    tiles = width // LANES
    n_mat = tiles // 2 + 1
    n_all = n_mat + tiles // 2
    half = width // 2
    rows = own.shape[-2]
    chips = width // rows
    chip = dp // 2 * nx + x

    def at(zz, yy, cc, xx):
        return ((zz * 2 + yy) * 2 + cc, xx)

    partner = at(z, y, other, x)
    y_peer = at(z, 1 - y, core, x)
    x_ids = [lax.rem(x + o, nx) for o in range(1, nx)]
    z_ids = [lax.rem(z + o, nz) for o in range(1, nz)]
    x_peers = [at(z, y, core, i) for i in x_ids]
    z_peers = [at(i, y, core, x) for i in z_ids]
    spread = [
        at(i // nx // 2, i // nx % 2, other, i % nx) for i in range(chips)
    ]
    peers = [y_peer] + x_peers + z_peers + spread

    barrier = pltpu.get_barrier_semaphore()
    for peer in peers:
        pl.semaphore_signal(barrier, inc=1, device_id=peer, device_id_type=MESH)
    pl.semaphore_wait(barrier, len(peers))

    count = [0]
    copies = []

    def send(src, dst, peer):
        n = count[0]
        count[0] += 1
        copy = pltpu.make_async_remote_copy(
            src_ref=src, dst_ref=dst, send_sem=send_sem.at[n], recv_sem=recv_sem.at[n],
            device_id=peer, device_id_type=MESH,
        )
        copy.start()
        copies.append(copy)
        return copy

    stack[0] = acts[...]
    stack[1] = grads[...]
    flipped[0] = acts[...].T
    flipped[1] = grads[...].T

    def term(role, chunk):
        if chunk < n_mat:
            pieces = []
            for i in range(tiles):
                j = (i + chunk) % tiles
                pieces.append(jnp.dot(
                    flipped[role, i * LANES:(i + 1) * LANES, :],
                    stack[role, :, j * LANES:(j + 1) * LANES],
                    preferred_element_type=jnp.float32,
                ))
            value = jnp.concatenate(pieces, axis=0)
        else:
            start = pl.multiple_of(role * half + (chunk - n_mat) * LANES, LANES)
            value = jnp.dot(
                flipped[1], stack[0, :, pl.ds(start, LANES)], preferred_element_type=jnp.float32
            )
        return value.reshape(own.shape[1:])

    waits = {}

    def core_send(c):
        outgoing[c] = term(other, c)
        waits[c] = [send(outgoing.at[c], incoming.at[c], partner)]
        own[c] = term(core, c)

    def arrived(c):
        for copy in waits[c]:
            copy.wait_recv()

    def first(c):
        arrived(c)
        own[c] = own[c] + incoming[c]
        k = c // 2
        if c % 2 == 0:
            waits[c] = [
                send(own.at[c, :, :, i], got_e1.at[k, s], peer)
                for s, (i, peer) in enumerate(zip(x_ids, x_peers))
            ]
        else:
            waits[c] = [send(own.at[c, :, 1 - y], got_o1.at[k], y_peer)]

    def second(c):
        arrived(c)
        k = c // 2
        if c % 2 == 0:
            total = own[c, :, :, x]
            for s in range(nx - 1):
                total = total + got_e1[k, s]
            sum_e[k] = total
            waits[c] = [send(sum_e.at[k, :, 1 - y], got_e2.at[k], y_peer)]
        else:
            sum_o[k] = own[c, :, y] + got_o1[k]
            waits[c] = [
                send(sum_o.at[k, :, i], got_o2.at[k, s], peer)
                for s, (i, peer) in enumerate(zip(x_ids, x_peers))
            ]

    def third(c):
        arrived(c)
        k = c // 2
        if c % 2 == 0:
            pair[c] = sum_e[k, :, y] + got_e2[k]
        else:
            total = sum_o[k, :, x]
            for s in range(nx - 1):
                total = total + got_o2[k, s]
            pair[c] = total
        waits[c] = [
            send(pair.at[c, i], got_z.at[c, s], peer)
            for s, (i, peer) in enumerate(zip(z_ids, z_peers))
        ]

    def fourth(c):
        arrived(c)
        total = pair[c, z]
        for s in range(nz - 1):
            total = total + got_z[c, s]
        mine[c] = total
        if c < n_mat:
            mat[c, z, y, x] = total
            spot = mat.at[c, z, y, x]
            waits[c] = [send(mine.at[c], spot, peer) for peer in z_peers]
        else:
            cross[c - n_mat, core] = total
            waits[c] = [send(mine.at[c], cross.at[c - n_mat, core], partner)]

    def fifth(c):
        arrived(c)
        if c >= n_mat:
            waits[c] = []
        elif c % 2 == 0:
            spot = mat.at[c, :, y, x]
            waits[c] = [send(spot, spot, y_peer)]
        else:
            spot = mat.at[c, :, y, x]
            waits[c] = [send(spot, spot, peer) for peer in x_peers]

    def sixth(c):
        arrived(c)
        if c >= n_mat:
            waits[c] = []
        elif c % 2 == 0:
            spot = mat.at[c, :, :, x]
            waits[c] = [send(spot, spot, peer) for peer in x_peers]
        else:
            spot = mat.at[c, :, y]
            waits[c] = [send(spot, spot, y_peer)]

    steps = [core_send, first, second, third, fourth, fifth, sixth, arrived]
    lag = 2
    for t in range(n_all + lag * len(steps)):
        for s, step in enumerate(steps):
            c = t - lag * s
            if 0 <= c < n_all:
                step(c)
    corner = (
        lax.broadcasted_iota(jnp.int32, (LANES, LANES), 0)
        == lax.broadcasted_iota(jnp.int32, (LANES, LANES), 1)
    ).astype(jnp.float32)
    damp = damping[core]

    def tile(i):
        return slice(i * LANES, (i + 1) * LANES)

    for c in range(n_mat):
        value = mat[c].reshape(width, LANES) * scale
        for i in range(tiles):
            piece = value[tile(i)]
            if c == 0:
                piece = piece + damp * corner
            j = (i + c) % tiles
            full[tile(i), tile(j)] = piece
            if 0 < c < tiles // 2:
                full[tile(j), tile(i)] = piece.T
    largest = jnp.max(jnp.sum(jnp.abs(full[...]), axis=0, keepdims=True), axis=1, keepdims=True)
    alpha = 1.0 / largest

    def parts(value):
        top = value.astype(jnp.bfloat16)
        return top, (value - top.astype(jnp.float32)).astype(jnp.bfloat16)

    for i in range(tiles):
        ids = lax.broadcasted_iota(jnp.int32, (LANES, width), 0) + i * LANES
        unit = (ids == lax.broadcasted_iota(jnp.int32, (LANES, width), 1)).astype(jnp.float32)
        high[0, tile(i)], low[0, tile(i)] = parts(unit - alpha * full[tile(i)])

    def mul(left, right):
        return jnp.dot(left, right, preferred_element_type=jnp.float32)

    @pl.loop(0, 2 * (width // PANEL))
    def _(n):
        k = n // (width // PANEL)
        cols = pl.ds(pl.multiple_of(lax.rem(n, width // PANEL) * PANEL, PANEL), PANEL)
        value = mul(low[k], high[k, :, cols]) + mul(high[k], low[k, :, cols])
        value = value + mul(high[k], high[k, :, cols])
        high[k + 1, :, cols], low[k + 1, :, cols] = parts(value)

    def apply_inverse():
        block[1] = block[0]

        @pl.loop(0, 5)
        def _(k):
            power = jnp.minimum(k, 2)
            value = block[1]
            top = value.astype(jnp.bfloat16).astype(jnp.float32)
            wide[...] = jnp.concatenate([top, value - top], axis=0).astype(jnp.bfloat16)

            @pl.loop(0, width // PANEL)
            def _(n):
                cols = pl.ds(pl.multiple_of(n * PANEL, PANEL), PANEL)
                both = mul(wide[...], high[power, :, cols])
                rest = mul(wide[...], low[power, :, cols])
                block[1, :, cols] = both[:rows] + (both[rows:] + rest[:rows])

            @pl.when(k != 3)
            def _():
                block[0] = block[0] + block[1]

            @pl.when(k < 3)
            def _():
                block[1] = block[0]

        block[0] = alpha * block[0]

    for c in range(n_all - n_mat):
        for h in range(2):
            start = h * half + c * LANES
            block[0, :, start:start + LANES] = cross[c, h] * scale
    apply_inverse()

    turned[...] = block[0].T.reshape(chips, rows, rows)
    turns = []
    for i, peer in enumerate(spread):
        turns.append(pltpu.make_async_remote_copy(
            src_ref=turned.at[i], dst_ref=landed.at[chip], send_sem=turn_send.at[i],
            recv_sem=turn_recv.at[chip], device_id=peer, device_id_type=MESH,
        ))
        turns[-1].start()
    for i in range(chips):
        pltpu.make_async_remote_copy(
            src_ref=turned.at[i], dst_ref=landed.at[i], send_sem=turn_send.at[i],
            recv_sem=turn_recv.at[i], device_id=spread[i], device_id_type=MESH,
        ).wait_recv()
    for i in range(chips):
        block[0, :, i * rows:(i + 1) * rows] = landed[i]
    apply_inverse()

    share = nx // 2
    span = width // nx
    slot = lax.rem(x, share)
    home = x // share

    for i in range(nx):
        parted[i] = block[0, :, i * span:(i + 1) * span]

    def part(o, where):
        i = lax.rem(x + o, nx)
        return pltpu.make_async_remote_copy(
            src_ref=parted.at[i], dst_ref=out.at[where], send_sem=part_send.at[o],
            recv_sem=part_recv.at[where], device_id=at(z, y, home if o else 0, i),
            device_id_type=MESH,
        )

    @pl.when(core == 1)
    def _():
        for o in range(1, nx):
            part(o, slot).start()

        @pl.when(home == 0)
        def _():
            part(0, slot).start()

        @pl.when(home == 1)
        def _():
            out[slot] = parted[x]

    for s in range(share):
        @pl.when(jnp.logical_or(core == 0, x != share + s))
        def _():
            part(1, s).wait_recv()

    @pl.when(core == 1)
    def _():
        for o in range(1, nx):
            part(o, slot).wait_send()

        @pl.when(home == 0)
        def _():
            part(0, slot).wait_send()

    for copy in copies + turns:
        copy.wait_send()


def local(acts, grads, damping):
    nz = lax.axis_size("dp") // 4
    nx = lax.axis_size("grp")
    tokens, width = acts.shape
    chips = 2 * nz * nx
    rows = width // chips
    tiles = width // LANES
    n_mat = tiles // 2 + 1
    n_half = tiles // 2
    n_all = n_mat + n_half
    even, odd = (n_all + 1) // 2, n_all // 2
    copies = n_all * (3 + 2 * (nx - 1) + 2 * (nz - 1) + 2)
    f32, bf16 = jnp.float32, jnp.bfloat16

    def room(*shape):
        return pltpu.VMEM(shape + (rows, LANES), f32)

    vmem = pl.BlockSpec(memory_space=pltpu.VMEM)
    out = pl.pallas_call(
        functools.partial(kernel, nz, nx, 1.0 / (tokens * 2 * chips)),
        out_shape=jax.ShapeDtypeStruct((nx // 2, rows, width // nx), f32),
        in_specs=[pl.BlockSpec(memory_space=pltpu.SMEM), vmem, vmem],
        out_specs=vmem,
        scratch_shapes=[
            room(n_mat, nz, 2, nx),
            room(n_half, 2),
            pltpu.VMEM((2, tokens, width), bf16),
            pltpu.VMEM((2, width, tokens), bf16),
            room(n_all, nz, 2, nx),
            room(n_all, nz, 2, nx),
            room(n_all, nz, 2, nx),
            room(even, nz, 2),
            room(odd, nz, nx),
            room(even, nx - 1, nz, 2),
            room(even, nz),
            room(odd, nz, nx),
            room(odd, nx - 1, nz),
            room(n_all, nz),
            room(n_all, nz - 1),
            room(n_all),
            pltpu.VMEM((width, width), f32),
            pltpu.VMEM((3, width, width), bf16),
            pltpu.VMEM((3, width, width), bf16),
            pltpu.VMEM((2, rows, width), f32),
            pltpu.VMEM((2 * rows, width), bf16),
            pltpu.VMEM((chips, rows, rows), f32),
            pltpu.VMEM((chips, rows, rows), f32),
            pltpu.VMEM((nx, rows, width // nx), f32),
            pltpu.SemaphoreType.DMA((copies,)),
            pltpu.SemaphoreType.DMA((copies,)),
            pltpu.SemaphoreType.DMA((chips,)),
            pltpu.SemaphoreType.DMA((chips,)),
            pltpu.SemaphoreType.DMA((nx,)),
            pltpu.SemaphoreType.DMA((nx // 2,)),
        ],
        compiler_params=pltpu.CompilerParams(
            collective_id=0, has_side_effects=True, vmem_limit_bytes=62 * 1024 * 1024
        ),
    )(damping, acts, grads)
    return out.reshape(nx // 2 * rows, width // nx)


def solution(mesh):
    placed = (P(("dp", "grp"), None), P(("dp", "grp"), None), P())
    return jax.shard_map(
        local, mesh=mesh, in_specs=placed, out_specs=P("dp", "grp"), check_vma=False
    )
```

profile of v0, /device:TPU:13, one launch (start us, length us, event | category | flops | bytes accessed | tf_op | source)
XLA Modules:
  0.0 125.7 jit_solution(6181926472227223677)
XLA Ops:
  0.0 124.1 %shard_map.37 = f32[1,64,512]{2,1,0:T(8,128)} custom-call(f32[2]{0:T(128)} %damping.1, bf16[512,1024]{1,0:T(8,128)(2,1)} %acts.1, bf16[512,1024]{1,0:T(8,128)(2,1)} %grads.1), custom_call_target="tpu_custom_call" | custom-call | tf_op jit(solution)/shard_map/pallas_call | solution.py:347
  124.1 1.6 %copy.5 = f32[64,512]{1,0:T(8,128)} copy(f32[64,512]{1,0:T(8,128)} %bitcast.1) | data formatting | bytes 262144
where the time goes:
time: 126 us
  Pallas kernels  124 us (98%)
  local copies, waits for them, and re-layouts  1.57 us (1%)
    pallas_call x1, Pallas kernels, local(): pl.pallas_call(functools.partial(kernel, nz, nx, 1.0 / (tokens * 2 * chip...  124 us

commit v1 on v0

--- a/solution.py
+++ b/solution.py
@@ -180,13 +180,6 @@
             spot = mat.at[c, :, y]
             waits[c] = [send(spot, spot, y_peer)]
 
-    steps = [core_send, first, second, third, fourth, fifth, sixth, arrived]
-    lag = 2
-    for t in range(n_all + lag * len(steps)):
-        for s, step in enumerate(steps):
-            c = t - lag * s
-            if 0 <= c < n_all:
-                step(c)
     corner = (
         lax.broadcasted_iota(jnp.int32, (LANES, LANES), 0)
         == lax.broadcasted_iota(jnp.int32, (LANES, LANES), 1)
@@ -196,7 +189,8 @@
     def tile(i):
         return slice(i * LANES, (i + 1) * LANES)
 
-    for c in range(n_mat):
+    def unpack(c):
+        arrived(c)
         value = mat[c].reshape(width, LANES) * scale
         for i in range(tiles):
             piece = value[tile(i)]
@@ -206,6 +200,20 @@
             full[tile(i), tile(j)] = piece
             if 0 < c < tiles // 2:
                 full[tile(j), tile(i)] = piece.T
+
+    steps = [core_send, first, second, third, fourth, fifth, sixth, unpack]
+    lag = 2
+    late = lag * 6 + 1
+    for t in range(n_mat + lag * len(steps)):
+        for s, step in enumerate(steps):
+            c = t - lag * s
+            if 0 <= c < n_mat:
+                step(c)
+        if n_mat <= t < n_all:
+            core_send(t)
+        if late <= t < late + n_all - n_mat:
+            first(t - late + n_mat)
+
     largest = jnp.max(jnp.sum(jnp.abs(full[...]), axis=0, keepdims=True), axis=1, keepdims=True)
     alpha = 1.0 / largest
 
@@ -221,13 +229,25 @@
     def mul(left, right):
         return jnp.dot(left, right, preferred_element_type=jnp.float32)
 
-    @pl.loop(0, 2 * (width // PANEL))
-    def _(n):
-        k = n // (width // PANEL)
-        cols = pl.ds(pl.multiple_of(lax.rem(n, width // PANEL) * PANEL, PANEL), PANEL)
-        value = mul(low[k], high[k, :, cols]) + mul(high[k], low[k, :, cols])
-        value = value + mul(high[k], high[k, :, cols])
-        high[k + 1, :, cols], low[k + 1, :, cols] = parts(value)
+    pending = [(step, c) for step in (second, third, fourth) for c in range(n_mat, n_all)]
+    panels = 2 * (width // PANEL)
+    for n in range(panels):
+        k, start = n // (width // PANEL), n % (width // PANEL) * PANEL
+        stop = start + PANEL
+        cols, below = slice(start, stop), slice(start, width)
+        value = mul(low[k, below], high[k, :, cols]) + mul(high[k, below], low[k, :, cols])
+        value = value + mul(high[k, below], high[k, :, cols])
+        top, rest = parts(value)
+        high[k + 1, below, cols], low[k + 1, below, cols] = top, rest
+        if stop < width:
+            high[k + 1, cols, stop:] = top[PANEL:].T
+            low[k + 1, cols, stop:] = rest[PANEL:].T
+        taken = -(-len(pending) // max(panels - 1 - n, 1))
+        for step, c in pending[:taken]:
+            step(c)
+        pending = pending[taken:]
+    for c in range(n_mat, n_all):
+        arrived(c)
 
     def apply_inverse():
         block[1] = block[0]

time: 126 us -> 138 us (1.095)
  Pallas kernels: 124 us -> 136 us
    pallas_call x1, Pallas kernels: 124 us -> 136 us  [local(): pl.pallas_call(functools.partial(kernel, nz, nx, 1.0 / (tokens * 2 * chip...]
where the time goes in v1:
time: 138 us; the launch traced here: 137 us
  Pallas kernels  136 us (99%)
  local copies, waits for them, and re-layouts  1.57 us (1%)
    pallas_call x1, Pallas kernels, local(): pl.pallas_call(functools.partial(kernel, nz, nx, 1.0 / (tokens * 2 * chip...  136 us

profile of v1, /device:TPU:13, one launch (start us, length us, event | category | flops | bytes accessed | tf_op | source)
XLA Modules:
  0.0 137.5 jit_solution(9623446619047890072)
XLA Ops:
  0.0 135.9 %shard_map.37 = f32[1,64,512]{2,1,0:T(8,128)} custom-call(f32[2]{0:T(128)} %damping.1, bf16[512,1024]{1,0:T(8,128)(2,1)} %acts.1, bf16[512,1024]{1,0:T(8,128)(2,1)} %grads.1), custom_call_target="tpu_custom_call" | custom-call | tf_op jit(solution)/shard_map/pallas_call | solution.py:367
  135.9 1.6 %copy.5 = f32[64,512]{1,0:T(8,128)} copy(f32[64,512]{1,0:T(8,128)} %bitcast.1) | data formatting | bytes 262144

commit v2 on v0

--- a/solution.py
+++ b/solution.py
@@ -221,13 +221,18 @@
     def mul(left, right):
         return jnp.dot(left, right, preferred_element_type=jnp.float32)
 
-    @pl.loop(0, 2 * (width // PANEL))
-    def _(n):
-        k = n // (width // PANEL)
-        cols = pl.ds(pl.multiple_of(lax.rem(n, width // PANEL) * PANEL, PANEL), PANEL)
-        value = mul(low[k], high[k, :, cols]) + mul(high[k], low[k, :, cols])
-        value = value + mul(high[k], high[k, :, cols])
-        high[k + 1, :, cols], low[k + 1, :, cols] = parts(value)
+    panels = 2 * (width // PANEL)
+    for n in range(panels):
+        k, start = n // (width // PANEL), n % (width // PANEL) * PANEL
+        stop = start + PANEL
+        cols, below = slice(start, stop), slice(start, width)
+        value = mul(low[k, below], high[k, :, cols]) + mul(high[k, below], low[k, :, cols])
+        value = value + mul(high[k, below], high[k, :, cols])
+        top, rest = parts(value)
+        high[k + 1, below, cols], low[k + 1, below, cols] = top, rest
+        if stop < width:
+            high[k + 1, cols, stop:] = top[PANEL:].T
+            low[k + 1, cols, stop:] = rest[PANEL:].T
 
     def apply_inverse():
         block[1] = block[0]

time: 126 us -> 119 us (0.944)
  Pallas kernels: 124 us -> 118 us
    pallas_call x1, Pallas kernels: 124 us -> 118 us  [local(): pl.pallas_call(functools.partial(kernel, nz, nx, 1.0 / (tokens * 2 * chip...]
where the time goes in v2:
time: 119 us
  Pallas kernels  118 us (99%)
  local copies, waits for them, and re-layouts  1.57 us (1%)
    pallas_call x1, Pallas kernels, local(): pl.pallas_call(functools.partial(kernel, nz, nx, 1.0 / (tokens * 2 * chip...  118 us

profile of v2, /device:TPU:13, one launch (start us, length us, event | category | flops | bytes accessed | tf_op | source)
XLA Modules:
  0.0 119.2 jit_solution(6528162133800134287)
XLA Ops:
  0.0 117.6 %shard_map.37 = f32[1,64,512]{2,1,0:T(8,128)} custom-call(f32[2]{0:T(128)} %damping.1, bf16[512,1024]{1,0:T(8,128)(2,1)} %acts.1, bf16[512,1024]{1,0:T(8,128)(2,1)} %grads.1), custom_call_target="tpu_custom_call" | custom-call | tf_op jit(solution)/shard_map/pallas_call | solution.py:352
  117.6 1.6 %copy.5 = f32[64,512]{1,0:T(8,128)} copy(f32[64,512]{1,0:T(8,128)} %bitcast.1) | data formatting | bytes 262144
